TPU v7x, 512 devices: a whole 4x4x16 slice. The times are simulated.
512 devices in a mesh: roll: 64 (over x, z_hi, y, core), kv: 8 (over z_lo).
Axes of the slice: x: 4, y: 4, z: 16 (z_hi: 2, z_lo: 8; z = z_hi * 8 + z_lo), core: 2. Of those that a mesh axis runs over, the one named last changes fastest.
Arguments:
- queries: bfloat16 [64, 4, 2048], P('roll', None, 'kv'), may hold values from -8 to 8
- prompt_cache: bfloat16 [4, 16384, 1024], P(None, 'roll', 'kv'), may hold values from -4 to 4
- gen_cache: bfloat16 [64, 128, 1024], P('roll', None, 'kv'), may hold values from -4 to 4
- gen_lengths: int32 [64], P('roll'), may hold values from 1 to 128, 4096 in all
- new_kv: bfloat16 [64, 4, 1024], P('roll', None, 'kv'), may hold values from -4 to 4
- w_out: bfloat16 [2048, 2880], P('kv'), may hold values from -3 to 3
- residual: bfloat16 [64, 4, 2880], P('roll', None, 'kv'), may hold values from -10 to 10
- norm_gain: float32 [2880], P('kv'), may hold values from 0.5 to 1.5
- w_gate: bfloat16 [64, 2880, 1440], P('roll', None, 'kv'), may hold values from -0.109375 to 0.109375
- w_up: bfloat16 [64, 2880, 1440], P('roll', None, 'kv'), may hold values from -0.109375 to 0.109375
- w_down: bfloat16 [64, 1440, 2880], P('roll', 'kv'), may hold values from -0.15625 to 0.15625
- expert_ids: int32 [64, 4, 4], replicated, may hold values from 0 to 63, all different within a row; in each aligned block of 256 rows (0 to 255, 256 to 511, ..., all dimensions but the last counted through in order) at most 48 rows name the same one
- route_weights: float32 [64, 4, 4], replicated, may hold values from 0.05 to 0.5
Outputs:
- layer_out: bfloat16 [64, 4, 2880], P('roll', None, 'kv')
Inputs may be any that keep to these rules, and one draw needn't show every extreme that they name: `expert_ids`: each row names 4 different experts; over all rows no expert is named more than 48 times, and one expert exactly 48 times. `gen_lengths`: the longest is exactly 128.
All inputs are finite; a program needn't handle non-finite values. No bound on the sum of `gen_lengths` on one device may be relied on, other than what follows from the above.
Results may differ from a plain program's by a relative error of at most 0.014.
Values may be sent and summed in bfloat16 or wider, within the bound.
A program may use at most 128 MiB of HBM per device.

v0:
```python
import jax
import jax.numpy as jnp
from jax import lax
from jax.sharding import PartitionSpec as P

D = 2880
HEAD = 64
TOPK = 4
MOSTE = 48


def merged(x, axis, combine):
    everything = jax.tree.map(lambda part: lax.all_gather(part, axis), x)
    initial = jax.tree.map(lambda part: part[0], everything)

    def hop(k, so_far):
        return combine(so_far, jax.tree.map(lambda part: part[k], everything))

    return lax.fori_loop(1, lax.axis_size(axis), hop, initial)


def merge_pair(left_part, right_part):
    maxima = jnp.maximum(left_part[0], right_part[0])
    left_factor = jnp.exp(left_part[0] - maxima)
    right_factor = jnp.exp(right_part[0] - maxima)
    totals = left_part[1] * left_factor + right_part[1] * right_factor
    accumulated = left_part[2] * left_factor[..., None] + right_part[2] * right_factor[..., None]
    return (maxima, totals, accumulated)


def on_device(
    queries,
    prompt_cache,
    gen_cache,
    gen_lengths,
    new_kv,
    w_out,
    residual,
    norm_gain,
    w_gate,
    w_up,
    w_down,
    expert_ids,
    route_weights,
):
    highest = lax.Precision.HIGHEST
    samp_local, step_count, query_width = queries.shape
    prompt_count, prompt_local, kv_width = prompt_cache.shape
    kv_local = kv_width // (2 * HEAD)
    per_group = query_width // (kv_local * HEAD)
    score_scale = HEAD ** (-0.5)
    roll_index = lax.axis_index("roll")
    everyone = lax.all_gather(queries, "roll", axis=0, tiled=True)
    group_size = everyone.shape[0] // prompt_count
    query_all = everyone.reshape(prompt_count, group_size, step_count, kv_local, per_group, HEAD)
    prompt_blocks = prompt_cache.reshape(prompt_count, prompt_local, kv_local, 2, HEAD)
    scores = (
        jnp.einsum(
            "pgtkrd,pnkd->pgtkrn",
            query_all,
            prompt_blocks[:, :, :, 0],
            preferred_element_type=jnp.float32,
        )
        * score_scale
    )
    maxima = jnp.max(scores, axis=-1)
    weights = jnp.exp(scores - maxima[..., None])
    totals = jnp.sum(weights, axis=-1)
    prompt_values = prompt_blocks[:, :, :, 1].astype(jnp.float32)
    accumulated = jnp.einsum("pgtkrn,pnkd->pgtkrd", weights, prompt_values, precision=highest)
    lead_shape = (prompt_count * group_size, step_count, kv_local, per_group)
    maxima = maxima.reshape(lead_shape)
    totals = totals.reshape(lead_shape)
    accumulated = accumulated.reshape(lead_shape + (HEAD,))
    maxima, totals, accumulated = merged((maxima, totals, accumulated), "roll", merge_pair)
    row_start = roll_index * samp_local
    maxima = lax.dynamic_slice_in_dim(maxima, row_start, samp_local, 0)
    totals = lax.dynamic_slice_in_dim(totals, row_start, samp_local, 0)
    accumulated = lax.dynamic_slice_in_dim(accumulated, row_start, samp_local, 0)
    own_query = queries.reshape(samp_local, step_count, kv_local, per_group, HEAD)
    gen_blocks = gen_cache.reshape(samp_local, -1, kv_local, 2, HEAD)
    gen_span = gen_blocks.shape[1]
    gen_scores = (
        jnp.einsum(
            "stkrd,snkd->stkrn",
            own_query,
            gen_blocks[:, :, :, 0],
            preferred_element_type=jnp.float32,
        )
        * score_scale
    )
    live_mask = jnp.arange(gen_span, dtype=jnp.int32)[None, :] < gen_lengths[:, None]
    gen_scores = jnp.where(live_mask[:, None, None, None, :], gen_scores, -jnp.inf)
    fresh_kv = new_kv.reshape(samp_local, step_count, kv_local, 2, HEAD)
    new_scores = (
        jnp.einsum(
            "stkrd,sukd->stkru", own_query, fresh_kv[:, :, :, 0], preferred_element_type=jnp.float32
        )
        * score_scale
    )
    causal = jnp.arange(step_count)[None, :] <= jnp.arange(step_count)[:, None]
    new_scores = jnp.where(causal[None, :, None, None, :], new_scores, -jnp.inf)
    overall = jnp.maximum(jnp.maximum(maxima, gen_scores.max(-1)), new_scores.max(-1))
    prompt_factor = jnp.exp(maxima - overall)
    gen_w = jnp.exp(gen_scores - overall[..., None])
    new_w = jnp.exp(new_scores - overall[..., None])
    denominator = totals * prompt_factor + gen_w.sum(-1) + new_w.sum(-1)
    numerator = accumulated * prompt_factor[..., None]
    numerator = numerator + jnp.einsum(
        "stkrn,snkd->stkrd", gen_w, gen_blocks[:, :, :, 1].astype(jnp.float32), precision=highest
    )
    numerator = numerator + jnp.einsum(
        "stkru,sukd->stkrd", new_w, fresh_kv[:, :, :, 1].astype(jnp.float32), precision=highest
    )
    local_rows = samp_local * step_count
    attended = (
        (numerator / denominator[..., None]).astype(jnp.bfloat16).reshape(local_rows, query_width)
    )
    projected = jnp.dot(attended, w_out, preferred_element_type=jnp.float32)
    projected = lax.psum_scatter(
        projected.astype(jnp.bfloat16), "kv", scatter_dimension=1, tiled=True
    ).astype(jnp.float32)
    residual_sum = residual.reshape(local_rows, -1).astype(jnp.float32) + projected
    squares = lax.psum(jnp.sum(residual_sum * residual_sum, axis=1), "kv")
    inverse = lax.rsqrt(squares / D + 1e-05)
    normed = (residual_sum * inverse[:, None] * norm_gain).astype(jnp.bfloat16)
    row_total = expert_ids.shape[0] * expert_ids.shape[1]
    route_ids = expert_ids.reshape(row_total, TOPK)
    route_w = route_weights.reshape(row_total, TOPK)
    matches = route_ids == roll_index
    present = jnp.any(matches, axis=1)
    row_weight = jnp.sum(jnp.where(matches, route_w, 0.0), axis=1)
    slot_of = jnp.cumsum(present.astype(jnp.int32)) - 1
    chooser = present[None, :] & (slot_of[None, :] == jnp.arange(MOSTE, dtype=jnp.int32)[:, None])
    select_half = chooser.astype(jnp.bfloat16)
    select_full = chooser.astype(jnp.float32)
    slot_weight = jnp.dot(select_full, row_weight, precision=highest)
    whole_rows = lax.all_gather(normed, "kv", axis=1, tiled=True)
    columns = select_half
    compact = jnp.dot(
        columns,
        lax.all_gather(whole_rows, "roll", axis=0, tiled=True),
        preferred_element_type=jnp.float32,
    ).astype(jnp.bfloat16)
    gate_pre = jnp.dot(compact, w_gate[0], preferred_element_type=jnp.float32)
    up_pre = jnp.dot(compact, w_up[0], preferred_element_type=jnp.float32)
    activation = (gate_pre * jax.nn.sigmoid(1.702 * gate_pre) * (up_pre + 1.0)).astype(jnp.bfloat16)
    expert_out = (
        jnp.dot(activation, w_down[0], preferred_element_type=jnp.float32) * slot_weight[:, None]
    )
    slot_sums = lax.psum_scatter(
        expert_out.astype(jnp.bfloat16), "kv", scatter_dimension=1, tiled=True
    ).astype(jnp.float32)
    columns = select_full
    expert_mix = lax.psum_scatter(
        lax.dot_general(columns, slot_sums, (((0,), (0,)), ((), ())), precision=highest),
        "roll",
        scatter_dimension=0,
        tiled=True,
    )
    return (residual_sum + expert_mix).astype(jnp.bfloat16).reshape(samp_local, step_count, -1)


def solution(mesh):
    in_specs = (
        P("roll", None, "kv"),
        P(None, "roll", "kv"),
        P("roll", None, "kv"),
        P("roll"),
        P("roll", None, "kv"),
        P("kv", None),
        P("roll", None, "kv"),
        P("kv"),
        P("roll", None, "kv"),
        P("roll", None, "kv"),
        P("roll", "kv", None),
        P(),
        P(),
    )
    out_specs = P("roll", None, "kv")
    return jax.shard_map(
        on_device, mesh=mesh, in_specs=in_specs, out_specs=out_specs, check_vma=False
    )
```

profile of v0, /device:TPU:32, one launch (start us, length us, event | category | flops | bytes accessed | tf_op | source)
XLA Modules:
  0.0 2215.5 jit_solution(90229492891172199)
XLA Ops:
  6.5 164.1 %all_gather.18 = bf16[64,4,256]{2,1,0:T(4,128)(2,1)S(1)} all-gather(bf16[1,4,256]{2,1,0:T(4,128)(2,1)} %param.15), channel_id=1, replica_groups=mesh['roll'=64,'kv'=8] {'roll'}, dimensions={0}, use_global_device_ids=true | all-gather | bytes 133120 | tf_op jit(solution)/shard_map/all_gather | solution.py:53
  175.6 1.3 dynamic-slice
  177.7 186.6 %all_gather.19 = f32[64,64,4,1,4]{1,4,3,2,0:T(4,128)S(1)} all-gather(f32[1,64,4,1,4]{1,4,3,2,0:T(4,128)S(1)} %all_gather_reshape.9), channel_id=1, replica_groups=mesh['roll'=64,'kv'=8] {'roll'}, dimensions={0}, use_global_device_ids=true | all-gather | bytes 266240 | tf_op jit(solution)/shard_map/all_gather | solution.py:13
  364.4 224.4 %all_gather.20 = f32[64,64,4,1,4]{1,4,3,2,0:T(4,128)} all-gather(f32[1,64,4,1,4]{1,4,3,2,0:T(4,128)S(1)} %bitcast.228), channel_id=1, replica_groups=mesh['roll'=64,'kv'=8] {'roll'}, dimensions={0}, use_global_device_ids=true | all-gather | bytes 266240 | tf_op jit(solution)/shard_map/all_gather | solution.py:13
  591.1 210.1 %while.19 = (s32[]{:T(128)}, f32[64,4,1,4]{0,3,2,1:T(4,128)S(1)}, f32[64,4,1,4]{0,3,2,1:T(4,128)S(1)}, f32[64,4,1,4,64]{4,3,2,1,0:T(4,128)S(1)}, f32[64,64,4,1,4...) while((s32[]{:T(128)}, f32[64,4,1,4]{0,3,2,1:T(4,128)S(1)}, ...), condition=%wide.region_3.0_spmd, body=%wide.region_2.0_spmd.sunk | while | flops 203781 | bytes 1388699 | solution.py:19
  609.9 1.2 fusion.76
  629.9 1.2 fusion.76
  649.9 1.2 fusion.76
  673.3 1.2 fusion.76
  693.3 1.2 fusion.76
  713.3 1.2 fusion.76
  736.6 1.2 fusion.76
  756.7 1.2 fusion.76
  802.9 52.3 %all-reduce = bf16[4,2880]{1,0:T(4,128)(2,1)S(1)} all-reduce(bf16[4,2880]{1,0:T(4,128)(2,1)S(1)} %convolution_convert_fusion.1), channel_id=2, replica_groups=mesh['roll'=64,'kv'=8] {'kv'}, use_global_device_ids=true, to_apply=%region_8.9.clone | all-reduce | flops 11520 | bytes 46080
  855.5 33.6 %psum.7 = f32[4]{0:T(128)S(1)} all-reduce(f32[4]{0:T(128)S(1)} %multiply_reduce_fusion), channel_id=1, replica_groups=mesh['roll'=64,'kv'=8] {'kv'}, use_global_device_ids=true, to_apply=%region_13.14 | all-reduce | flops 4 | bytes 32 | tf_op jit(solution)/shard_map/psum | solution.py:124
  889.2 39.5 %all-gather = bf16[8,360,4]{1,2,0:T(4,128)(2,1)S(1)} all-gather(bf16[1,360,4]{1,2,0:T(4,128)(2,1)S(1)} %fusion.52), channel_id=1, replica_groups=mesh['roll'=64,'kv'=8] {'kv'}, dimensions={0}, use_global_device_ids=true | all-gather | bytes 25920 | tf_op jit(solution)/shard_map/all_gather | solution.py:138
  930.9 106.3 %all-gather.7.cloned.1.call-done = bf16[64,4,2880]{2,1,0:T(4,128)(2,1)} async-done(((bf16[1,4,2880]{2,1,0:T(4,128)(2,1)}), bf16[64,4,2880]{2,1,0:T(4,128)(2,1)}) %all-gather.7.cloned.1.call-update) | async-done | bytes 1474576 | tf_op jit(solution)/shard_map/all_gather | solution.py:142
  1037.3 2.6 reshape.214
  1042.4 2.9 fusion.6
  1045.4 106.2 %all-reduce.6.cloned.1.call-done = bf16[48,2880]{1,0:T(8,128)(2,1)} async-done(((bf16[48,2880]{1,0:T(8,128)(2,1)}), bf16[48,2880]{1,0:T(8,128)(2,1)}) %all-reduce.6.cloned.1.call-update) | async-done | bytes 276496
  1151.6 1.8 fusion.33
  1153.5 1.3 dynamic-slice.4
  1155.4 1052.2 %all-reduce.8.cloned.1.call-done = f32[256,360]{1,0:T(8,128)} async-done(((f32[256,360]{1,0:T(8,128)}), f32[256,360]{1,0:T(8,128)}) %all-reduce.8.cloned.1.call-update) | async-done | bytes 368656
  2207.6 1.4 fusion.53
  (518 shorter events, 210.0 us)
Async XLA Ops:
  6.5 795.9 %copy-start = (bf16[256,2880]{0,1:T(8,128)(2,1)S(1)}, bf16[256,2880]{0,1:T(8,128)(2,1)}, u32[]{:S(2)}) copy-start(bf16[256,2880]{0,1:T(8,128)(2,1)} %param.20) | copy-start | bytes 4423684
  6.5 583.1 %all-gather.5.cloned.1.call-start = ((), (), s32[]{:S(2)}) async-start(), calls=%async_computation | async-start | bytes 34078720 | tf_op jit(solution)/shard_map/all_gather | solution.py:13
  173.0 1.0 copy-start.5
  173.9 0.8 copy-start.9
  173.9 0.9 copy-start.3
  173.9 863.4 %all-gather.7.cloned.1.call-start = ((), (), s32[]{:S(2)}) async-start(), calls=%async_computation.1 | async-start | bytes 1530880 | tf_op jit(solution)/shard_map/all_gather | solution.py:142
  801.2 54.0 %copy-start.4 = (bf16[1,4,360]{2,1,0:T(4,128)(2,1)S(1)}, bf16[1,4,360]{2,1,0:T(4,128)(2,1)}, u32[]{:S(2)}) copy-start(bf16[1,4,360]{2,1,0:T(4,128)(2,1)} %param.21) | copy-start | bytes 8644
  801.2 87.9 %copy-start.8 = (f32[360]{0:T(512)S(1)}, f32[360]{0:T(512)}, u32[]{:S(2)}) copy-start(f32[360]{0:T(512)} %param.22) | copy-start | bytes 4324
  801.4 128.1 %copy-start.6 = (f32[64,4,4]{0,2,1:T(4,128)S(1)}, f32[64,4,4]{0,2,1:T(4,128)}, u32[]{:S(2)}) copy-start(f32[64,4,4]{0,2,1:T(4,128)} %param.27) | copy-start | bytes 12292
  801.4 128.1 %copy-start.7 = (s32[64,4,4]{0,2,1:T(4,128)S(1)}, s32[64,4,4]{0,2,1:T(4,128)}, u32[]{:S(2)}) copy-start(s32[64,4,4]{0,2,1:T(4,128)} %param.26) | copy-start | bytes 12292
  929.4 222.2 %all-reduce.6.cloned.1.call-start = ((), (), s32[]{:S(2)}) async-start(), calls=%async_computation.2 | async-start | bytes 565248
  1039.9 1.2 copy-start.2
  1041.2 1.2 copy-start.1
  1045.3 1162.3 %all-reduce.8.cloned.1.call-start = ((), (), s32[]{:S(2)}) async-start(), calls=%async_computation.3 | async-start | bytes 786432
Sparse Core Ops, SparseCore 0:
  174.0 408.0 all-gather.4
  929.6 107.6 all-gather.6
  1045.5 106.0 all-reduce.5
  1154.6 1052.9 all-reduce.7
where the time goes:
time: 2220 us
  waiting for transfers between devices  1260 us (57%)
  blocking collectives  701 us (32%)
  other arithmetic  124 us (6%)
  local copies, waits for them, and re-layouts  98.2 us (4%)
    unnamed x6, waiting for transfers between devices  1160 us
    all_gather x2, blocking collectives, merged(): everything = jax.tree.map(lambda part: lax.all_gather(part, axis), x)  411 us
    all_gather x1, blocking collectives, on_device(): everyone = lax.all_gather(queries, 'roll', axis=0, tiled=True)  164 us
    all_gather x1, waiting for transfers between devices, on_device(): lax.all_gather(whole_rows, 'roll', axis=0, tiled=True)  106 us
    add x63, other arithmetic, merge_pair(): left_part[2] * left_factor[..., None]  74.7 us
    dynamic_slice x63, local copies, waits for them, and re-layouts, hop(): return combine(so_far, jax.tree.map(lambda part: part[k], everything))  68.2 us
    unnamed x1, blocking collectives  52.3 us
    mul x63, other arithmetic, merge_pair(): right_part[2] * right_factor[..., None]  45.8 us
  transfers between devices with their start and end apart: 4, of which 3 were waited for; matrix products, arithmetic and copies ran while one was open for 0% of the time, Pallas kernels for 0%

commit v1 on v0

--- a/solution.py
+++ b/solution.py
@@ -50,7 +50,9 @@
     per_group = query_width // (kv_local * HEAD)
     score_scale = HEAD ** (-0.5)
     roll_index = lax.axis_index("roll")
-    everyone = lax.all_gather(queries, "roll", axis=0, tiled=True)
+    everyone = jnp.concatenate(
+        lax.all_to_all(jnp.stack([queries] * lax.axis_size("roll")), "roll", 0, 0), axis=0
+    )
     group_size = everyone.shape[0] // prompt_count
     query_all = everyone.reshape(prompt_count, group_size, step_count, kv_local, per_group, HEAD)
     prompt_blocks = prompt_cache.reshape(prompt_count, prompt_local, kv_local, 2, HEAD)

time: 2220 us -> 2100 us (0.946)
  blocking collectives: 701 us -> 515 us
  waiting for transfers between devices: 1260 us -> 1300 us
    all_gather x1 -> x0, blocking collectives: 164 us -> none  [on_device(): everyone = lax.all_gather(queries, 'roll', axis=0, tiled=True)]
    all_gather x2, blocking collectives: 411 us -> 362 us  [merged(): everything = jax.tree.map(lambda part: lax.all_gather(part, axis), x)]
    unnamed x1, blocking collectives: 52.3 us -> 81.5 us
    all_gather x1, waiting for transfers between devices: 0.01 us -> 24.3 us  [merged(): everything = jax.tree.map(lambda part: lax.all_gather(part, axis), x)]
  transfers between devices with their start and end apart: 4 -> 5, of which waited for: 3 -> 5; matrix products, arithmetic and copies ran while one was open for 0% -> 0% of each run, Pallas kernels for 0% -> 0%
where the time goes in v1:
time: 2100 us; the launch traced here: 2090 us
  waiting for transfers between devices  1300 us (62%)
  blocking collectives  515 us (25%)
  other arithmetic  125 us (6%)
  local copies, waits for them, and re-layouts  99.7 us (5%)
    unnamed x6, waiting for transfers between devices  1160 us
    all_gather x2, blocking collectives, merged(): everything = jax.tree.map(lambda part: lax.all_gather(part, axis), x)  362 us
    all_gather x1, waiting for transfers between devices, on_device(): lax.all_gather(whole_rows, 'roll', axis=0, tiled=True)  101 us
    unnamed x1, blocking collectives  81.5 us
    add x63, other arithmetic, merge_pair(): left_part[2] * left_factor[..., None]  75 us
    dynamic_slice x63, local copies, waits for them, and re-layouts, hop(): return combine(so_far, jax.tree.map(lambda part: part[k], everything))  68.2 us
    mul x63, other arithmetic, merge_pair(): right_part[2] * right_factor[..., None]  45.8 us
  transfers between devices with their start and end apart: 5, of which 5 were waited for; matrix products, arithmetic and copies ran while one was open for 0% of the time, Pallas kernels for 0%

profile of v1, /device:TPU:32, one launch (start us, length us, event | category | flops | bytes accessed | tf_op | source)
XLA Modules:
  0.0 2091.7 jit_solution(7596711583473457345)
XLA Ops:
  6.5 1.5 stack.2
  8.0 20.3 all-to-all-start
  29.4 20.2 all-to-all-done
  53.0 1.3 dynamic-slice
  56.0 175.0 %all_gather.15 = f32[64,64,4,1,4]{1,4,3,2,0:T(4,128)S(1)} all-gather(f32[1,64,4,1,4]{1,4,3,2,0:T(4,128)S(1)} %all_gather_reshape.9), channel_id=1, replica_groups=mesh['roll'=64,'kv'=8] {'roll'}, dimensions={0}, use_global_device_ids=true | all-gather | bytes 266240 | tf_op jit(solution)/shard_map/all_gather | solution.py:13
  231.0 187.0 %all_gather.16 = f32[64,64,4,1,4]{1,4,3,2,0:T(4,128)} all-gather(f32[1,64,4,1,4]{1,4,3,2,0:T(4,128)S(1)} %bitcast.229), channel_id=1, replica_groups=mesh['roll'=64,'kv'=8] {'roll'}, dimensions={0}, use_global_device_ids=true | all-gather | bytes 266240 | tf_op jit(solution)/shard_map/all_gather | solution.py:13
  418.8 24.3 %all-gather.5.cloned.1.call-done = f32[64,64,4,1,4,64]{5,1,4,3,2,0:T(8,128)} async-done(((f32[1,64,4,1,4,64]{5,1,4,3,2,0:T(8,128)}), f32[64,64,4,1,4,64]{5,1,4,3,2,0:T(8,128)}) %all-gather.5.cloned.1.call-update) | async-done | bytes 16777232 | tf_op jit(solution)/shard_map/all_gather | solution.py:13
  444.5 210.5 %while.19 = (s32[]{:T(128)}, f32[64,4,1,4]{0,3,2,1:T(4,128)S(1)}, f32[64,4,1,4]{0,3,2,1:T(4,128)S(1)}, f32[64,4,1,4,64]{4,3,2,1,0:T(4,128)S(1)}, f32[64,64,4,1,4...) while((s32[]{:T(128)}, f32[64,4,1,4]{0,3,2,1:T(4,128)S(1)}, ...), condition=%wide.region_3.0_spmd, body=%wide.region_2.0_spmd.sunk | while | flops 203781 | bytes 1388699 | solution.py:19
  456.6 1.2 fusion.76
  466.7 1.2 fusion.76
  476.7 1.2 fusion.76
  486.7 1.2 fusion.76
  496.7 1.2 fusion.76
  656.6 81.5 %all-reduce = bf16[4,2880]{1,0:T(4,128)(2,1)S(1)} all-reduce(bf16[4,2880]{1,0:T(4,128)(2,1)S(1)} %convolution_convert_fusion.1), channel_id=2, replica_groups=mesh['roll'=64,'kv'=8] {'kv'}, use_global_device_ids=true, to_apply=%region_8.9.clone | all-reduce | flops 11520 | bytes 46080
  738.3 31.8 %psum.7 = f32[4]{0:T(128)S(1)} all-reduce(f32[4]{0:T(128)S(1)} %multiply_reduce_fusion), channel_id=1, replica_groups=mesh['roll'=64,'kv'=8] {'kv'}, use_global_device_ids=true, to_apply=%region_13.14 | all-reduce | flops 4 | bytes 32 | tf_op jit(solution)/shard_map/psum | solution.py:126
  770.2 39.5 %all-gather = bf16[8,360,4]{1,2,0:T(4,128)(2,1)S(1)} all-gather(bf16[1,360,4]{1,2,0:T(4,128)(2,1)S(1)} %fusion.52), channel_id=1, replica_groups=mesh['roll'=64,'kv'=8] {'kv'}, dimensions={0}, use_global_device_ids=true | all-gather | bytes 25920 | tf_op jit(solution)/shard_map/all_gather | solution.py:140
  812.0 101.5 %all-gather.7.cloned.1.call-done = bf16[64,4,2880]{2,1,0:T(4,128)(2,1)} async-done(((bf16[1,4,2880]{2,1,0:T(4,128)(2,1)}), bf16[64,4,2880]{2,1,0:T(4,128)(2,1)}) %all-gather.7.cloned.1.call-update) | async-done | bytes 1474576 | tf_op jit(solution)/shard_map/all_gather | solution.py:144
  913.5 2.6 reshape.216
  918.6 2.9 fusion.6
  921.6 106.2 %all-reduce.6.cloned.1.call-done = bf16[48,2880]{1,0:T(8,128)(2,1)} async-done(((bf16[48,2880]{1,0:T(8,128)(2,1)}), bf16[48,2880]{1,0:T(8,128)(2,1)}) %all-reduce.6.cloned.1.call-update) | async-done | bytes 276496
  1027.8 1.8 fusion.33
  1029.7 1.3 dynamic-slice.4
  1031.6 1052.2 %all-reduce.8.cloned.1.call-done = f32[256,360]{1,0:T(8,128)} async-done(((f32[256,360]{1,0:T(8,128)}), f32[256,360]{1,0:T(8,128)}) %all-reduce.8.cloned.1.call-update) | async-done | bytes 368656
  2083.8 1.4 fusion.53
  (520 shorter events, 214.0 us)
Async XLA Ops:
  6.5 649.6 %copy-start = (bf16[256,2880]{0,1:T(8,128)(2,1)S(1)}, bf16[256,2880]{0,1:T(8,128)(2,1)}, u32[]{:S(2)}) copy-start(bf16[256,2880]{0,1:T(8,128)(2,1)} %param.20) | copy-start | bytes 4423684
  8.0 41.7 %all-to-all-start = ((bf16[64,1,4,256]{3,2,1,0:T(4,128)(2,1)}), bf16[64,1,4,256]{3,2,1,0:T(4,128)(2,1)S(1)}, u32[]{:S(2)}, u32[]{:S(2)}) async-start(bf16[64,1,4,256]{3,2,1,0:T(4,128)(2,1)} %stack.2), calls=%async_computation | async-start | bytes 262144 | tf_op jit(solution)/shard_map/all_to_all | solution.py:54
  28.3 414.7 %all-gather.5.cloned.1.call-start = ((), (), s32[]{:S(2)}) async-start(), calls=%async_computation.1 | async-start | bytes 34078720 | tf_op jit(solution)/shard_map/all_gather | solution.py:13
  51.0 1.0 copy-start.5
  51.0 1.1 copy-start.9
  51.0 1.1 copy-start.3
  51.9 861.6 %all-gather.7.cloned.1.call-start = ((), (), s32[]{:S(2)}) async-start(), calls=%async_computation.2 | async-start | bytes 1530880 | tf_op jit(solution)/shard_map/all_gather | solution.py:144
  654.9 83.2 %copy-start.4 = (bf16[1,4,360]{2,1,0:T(4,128)(2,1)S(1)}, bf16[1,4,360]{2,1,0:T(4,128)(2,1)}, u32[]{:S(2)}) copy-start(bf16[1,4,360]{2,1,0:T(4,128)(2,1)} %param.21) | copy-start | bytes 8644
  654.9 115.2 %copy-start.8 = (f32[360]{0:T(512)S(1)}, f32[360]{0:T(512)}, u32[]{:S(2)}) copy-start(f32[360]{0:T(512)} %param.22) | copy-start | bytes 4324
  655.1 155.5 %copy-start.6 = (f32[64,4,4]{0,2,1:T(4,128)S(1)}, f32[64,4,4]{0,2,1:T(4,128)}, u32[]{:S(2)}) copy-start(f32[64,4,4]{0,2,1:T(4,128)} %param.27) | copy-start | bytes 12292
  655.1 155.5 %copy-start.7 = (s32[64,4,4]{0,2,1:T(4,128)S(1)}, s32[64,4,4]{0,2,1:T(4,128)}, u32[]{:S(2)}) copy-start(s32[64,4,4]{0,2,1:T(4,128)} %param.26) | copy-start | bytes 12292
  810.5 217.3 %all-reduce.6.cloned.1.call-start = ((), (), s32[]{:S(2)}) async-start(), calls=%async_computation.3 | async-start | bytes 565248
  916.2 1.2 copy-start.2
  917.4 1.2 copy-start.1
  921.6 1162.3 %all-reduce.8.cloned.1.call-start = ((), (), s32[]{:S(2)}) async-start(), calls=%async_computation.4 | async-start | bytes 786432
Sparse Core Ops, SparseCore 0:
  52.1 390.9 all-gather.4
  810.6 102.8 all-gather.6
  921.7 106.0 all-reduce.5
  1030.9 1052.9 all-reduce.7
